TPU v7x, 512 devices: a whole 4x8x8 slice. The times are simulated.
512 devices in a mesh: tm: 32 (over z, x), tile: 16 (over y, core).
Axes of the slice: x: 4, y: 8, z: 8, core: 2. Of those that a mesh axis runs over, the one named last changes fastest.
Arguments:
- features: bfloat16 [32, 32, 160, 512], P('tm', 'tile'), may hold values from -200 to 200, as said below
- norm_gain: float32 [512], replicated, may hold values from 0.1 to 1.9
- query_weight: bfloat16 [512, 512], replicated, may hold values from -7.9991455 to 7.9991455, as said below
- key_weight: bfloat16 [512, 512], replicated, may hold values from -0.25 to 0.25
- value_weight: bfloat16 [512, 512], replicated, may hold values from -0.25 to 0.25
- out_weight: bfloat16 [512, 512], replicated, may hold values from -0.5 to 0.5
- conv_weight: bfloat16 [3, 3, 3, 512, 256], replicated, may hold values from -0.0546875 to 0.0546875
- skip_weight: bfloat16 [512, 256], replicated, may hold values from -0.125 to 0.125
Outputs:
- decoded: bfloat16 [64, 32, 160, 256], P('tm', 'tile')
Inputs may be any that keep to these rules, and one draw needn't show every extreme that they name: Latent features whose magnitude varies from row to row and column to column. `query_weight`: A dense projection matrix.
All inputs are finite; a program needn't handle non-finite values.
Results may differ from a plain program's by a relative error of at most 0.012.
The roundings to bfloat16 on the way count: a program that leaves them out, or rounds other values in their place, can miss the bound.
Values may be sent and summed in bfloat16 or wider, within the bound.
A program may use at most 128 MiB of HBM per device.

v0:
```python
import jax
import jax.numpy as jnp
from jax import lax
from jax.sharding import PartitionSpec as P

GROUPS = 32


def shifted(array, axis, by):
    devices = lax.axis_size(axis)
    pairs = [(i, i + by) for i in range(devices) if 0 <= i + by < devices]
    return lax.ppermute(array, axis, pairs)


def padded_2(block, sides, width):
    for axis, dim in sides:
        count = lax.axis_size(axis)
        forward = [(i, i + 1) for i in range(count - 1)]
        backward = [(target, source) for source, target in forward]
        low = lax.ppermute(
            lax.slice_in_dim(block, block.shape[dim] - width, None, axis=dim), axis, forward
        )
        high = lax.ppermute(lax.slice_in_dim(block, 0, width, axis=dim), axis, backward)
        block = jnp.concatenate([low, block, high], axis=dim)
    return block


def per_device(
    features,
    norm_gain,
    query_weight,
    key_weight,
    value_weight,
    out_weight,
    conv_weight,
    skip_weight,
):
    frames, tile_rows, tile_cols, channels = features.shape
    cell_count = tile_rows * tile_cols
    group_width = channels // GROUPS
    grouped = features.astype(jnp.float32).reshape(frames, cell_count, GROUPS, group_width)
    total, squared = lax.psum(
        (jnp.sum(grouped, axis=(1, 3)), jnp.sum(grouped * grouped, axis=(1, 3))), "tile"
    )
    population = lax.axis_size("tile") * cell_count * group_width
    mean = (total / population)[:, None, :, None]
    var = (squared / population)[:, None, :, None] - mean * mean
    normed = ((grouped - mean) * lax.rsqrt(var + 1e-06)).reshape(
        frames, cell_count, channels
    ) * norm_gain
    normed = normed.astype(jnp.bfloat16)
    queries = jnp.einsum(
        "fnc,cd->fnd", normed, query_weight, preferred_element_type=jnp.float32
    ).astype(jnp.bfloat16)
    key_local = jnp.einsum(
        "fnc,cd->fnd", normed, key_weight, preferred_element_type=jnp.float32
    ).astype(jnp.bfloat16)
    value_local = jnp.einsum(
        "fnc,cd->fnd", normed, value_weight, preferred_element_type=jnp.float32
    ).astype(jnp.bfloat16)
    key_rows, value_rows = (
        lax.all_gather(key_local, "tile", axis=1, tiled=True),
        lax.all_gather(value_local, "tile", axis=1, tiled=True),
    )
    scores = jnp.einsum(
        "fqc,fkc->fqk", queries, key_rows, preferred_element_type=jnp.float32
    ) * channels ** (-0.5)
    peak = jnp.max(scores, axis=2, keepdims=True)
    unnormed = jnp.exp(scores - peak)
    denominator = jnp.sum(unnormed, axis=2, keepdims=True)
    weights = unnormed.astype(jnp.bfloat16)
    attended = (
        jnp.einsum("fqk,fkc->fqc", weights, value_rows, preferred_element_type=jnp.float32)
        / denominator
    ).astype(jnp.bfloat16)
    change = jnp.einsum("fqc,cd->fqd", attended, out_weight, preferred_element_type=jnp.float32)
    mid = (features.astype(jnp.float32).reshape(frames, cell_count, channels) + change).astype(
        jnp.bfloat16
    )
    act = (
        jax.nn.silu(mid.astype(jnp.float32))
        .astype(jnp.bfloat16)
        .reshape(frames, tile_rows, tile_cols, channels)
    )
    first_span = lax.axis_index("tm") == 0
    arrived = shifted(act, "tm", 1)
    arrived = jnp.where(first_span, act, arrived)
    stacked = jnp.concatenate([arrived, act], axis=0)
    rimmed = padded_2(stacked, (("tile", 1),), 1)
    padded = jnp.pad(rimmed, ((0, 0), (0, 0), (1, 1), (0, 0)))
    pieces = [
        padded[:, offset_y : offset_y + tile_rows, offset_x : offset_x + tile_cols, :]
        for offset_y in range(3)
        for offset_x in range(3)
    ]
    patches = jnp.concatenate(pieces, axis=-1).reshape(frames + 1, cell_count, 9 * channels)
    patch_before = patches[:-1]
    patch_now = patches[1:]
    taps = conv_weight.reshape(3, 9 * channels, conv_weight.shape[-1])
    skip = jnp.einsum("fnc,cd->fnd", mid, skip_weight, preferred_element_type=jnp.float32)
    first_tap = jnp.einsum("fnc,cd->fnd", patch_before, taps[0], preferred_element_type=jnp.float32)
    even = (
        first_tap
        + jnp.einsum("fnc,cd->fnd", patch_before, taps[1], preferred_element_type=jnp.float32)
        + jnp.einsum("fnc,cd->fnd", patch_now, taps[2], preferred_element_type=jnp.float32)
        + skip
    )
    odd = (
        first_tap
        + jnp.einsum("fnc,cd->fnd", patch_now, taps[1], preferred_element_type=jnp.float32)
        + jnp.einsum("fnc,cd->fnd", patch_now, taps[2], preferred_element_type=jnp.float32)
        + skip
    )
    decoded = jnp.stack([even, odd], axis=1).astype(jnp.bfloat16)
    return decoded.reshape(2 * frames, tile_rows, tile_cols, conv_weight.shape[-1])


def solution(mesh):
    in_specs = (P("tm", "tile", None, None), P(), P(), P(), P(), P(), P(), P())
    out_specs = P("tm", "tile", None, None)
    return jax.shard_map(
        per_device, mesh=mesh, in_specs=in_specs, out_specs=out_specs, check_vma=False
    )
```

profile of v0, /device:TPU:65, one launch (start us, length us, event | category | flops | bytes accessed | tf_op | source)
XLA Modules:
  0.0 177.7 jit_solution(7068608001065423834)
XLA Ops:
  6.5 1.1 convert_reduce_fusion
  8.1 24.2 %all-reduce.1 = (f32[1,32]{1,0:T(1,128)S(1)}, f32[1,32]{1,0:T(1,128)S(1)}) all-reduce(f32[1,32]{1,0:T(1,128)S(1)} %bitcast.67, f32[1,32]{1,0:T(1,128)S(1)} %bitcast.66), channel_id=1, replica_groups=mesh['tm'=32,'tile'=16] {'tile'}, use_global_device_ids=true, to_apply=%region_5.0 | all-reduce | flops 64 | bytes 512 | tf_op jit(solution)/shard_map/psum | solution.py:42
  32.6 1.1 fusion.33
  33.7 2.1 %convolution_convert_fusion.1 = bf16[320,512]{1,0:T(8,128)(2,1)} fusion(bf16[320,512]{1,0:T(8,128)(2,1)S(1)} %fusion.33, bf16[512,512]{1,0:T(8,128)(2,1)} %param.11), kind=kOutput, calls=%fused_computation.17 | convolution fusion | flops 167936000 | bytes 1179648 | tf_op jit(solution)/shard_map/fnc,cd->fnd/dot_general | solution.py:55
  35.9 2.1 %convolution_convert_fusion = bf16[320,512]{1,0:T(8,128)(2,1)} fusion(bf16[320,512]{1,0:T(8,128)(2,1)S(1)} %fusion.33, bf16[512,512]{1,0:T(8,128)(2,1)} %param.12), kind=kOutput, calls=%fused_computation.16 | convolution fusion | flops 167936000 | bytes 1179648 | tf_op jit(solution)/shard_map/fnc,cd->fnd/dot_general | solution.py:58
  38.0 47.5 %all-gather.5.cloned.1.call-done = bf16[5120,512]{1,0:T(8,128)(2,1)} async-done(((bf16[320,512]{1,0:T(8,128)(2,1)}), bf16[5120,512]{1,0:T(8,128)(2,1)}) %all-gather.5.cloned.1.call-update) | async-done | bytes 5242896 | tf_op jit(solution)/shard_map/all_gather | solution.py:62
  85.5 7.3 %fusion.41 = (f32[320]{0:T(512)S(1)}, f32[320,5120]{1,0:T(8,128)}) fusion(bf16[5120,512]{1,0:T(8,128)(2,1)} %all-gather.5.cloned.1.call-done, bf16[320,512]{1,0:T(8,128)(2,1)S(1)} %fusion.33, bf16[512,512]{1,0:T(8,128)(2,1)S(1)} %copy-done), kind=kOutput, calls=%fused_computation.70 | convolution fusion | flops 1848934144 | bytes 12649728 | tf_op jit(solution)/shard_map/fqc,fkc->fqk/dot_general | solution.py:65
  92.8 4.0 %fusion = f32[320]{0:T(512)S(1)} fusion(f32[320,5120]{1,0:T(8,128)} %get-tuple-element.17, f32[320]{0:T(512)S(1)} %get-tuple-element.16), kind=kLoop, calls=%fused_computation.2 | loop fusion | flops 3276480 | bytes 6556160 | tf_op jit(solution)/shard_map/reduce_sum | solution.py:70
  96.8 35.6 %all-gather.7.cloned.1.call-done = bf16[5120,512]{1,0:T(8,128)(2,1)} async-done(((bf16[320,512]{1,0:T(8,128)(2,1)}), bf16[5120,512]{1,0:T(8,128)(2,1)}) %all-gather.7.cloned.1.call-update) | async-done | bytes 5242896 | tf_op jit(solution)/shard_map/all_gather | solution.py:63
  132.4 6.6 %fusion.27 = (bf16[320,512]{1,0:T(8,128)(2,1)S(1)}, bf16[320,512]{1,0:T(8,128)(2,1)S(1)}) fusion(bf16[512,512]{1,0:T(8,128)(2,1)S(1)} %copy-done.3, bf16[5120,512]{1,0:T(8,128)(2,1)} %all-gather.7.cloned.1.call-done, f32[320,5120]{1,0:T(8,128)} %get-tuple-element.17, f32[320]{0:T(512)S(1)} %get-tuple-element.16, f32[320]{0:T(512)S(1)} %fusion, ...), kind=kOutput, calls=%fused_computation.39 | convolution fusion | flops 1850572800 | bytes 13306368 | tf_op jit(solution)/shard_map/fqc,cd->fqd/dot_general | solution.py:76
  139.0 3.1 %collective-permute-start = (bf16[1,2,160,512]{3,2,1,0:T(8,128)(2,1)S(1)}, bf16[1,2,160,512]{3,2,1,0:T(8,128)(2,1)S(1)}, u32[]{:S(2)}, u32[]{:S(2)}) collective-permute-start(bf16[1,2,160,512]{3,2,1,0:T(8,128)(2,1)S(1)} %bitcast.54), channel_id=1, source_target_pairs={{0,16},{16,32},{32,48},{48,64},{64,80},{80,96},{96,112},{112,128},... | collective-permute-start | bytes 983048 | tf_op jit(solution)/shard_map/ppermute | solution.py:12
  142.1 10.0 %collective-permute-done = bf16[1,2,160,512]{3,2,1,0:T(8,128)(2,1)S(1)} collective-permute-done((bf16[1,2,160,512]{3,2,1,0:T(8,128)(2,1)S(1)}, bf16[1,2,160,512]{3,2,1,0:T(8,128)(2,1)S(1)}, u32[]{:S(2)}, u32[]{:S(2)}) %collective-permute-start) | collective-permute-done | bytes 327712 | tf_op jit(solution)/shard_map/ppermute | solution.py:12
  152.2 4.0 %collective-permute-start.1 = (bf16[2,1,160,512]{3,2,1,0:T(8,128)(2,1)S(1)}, bf16[2,1,160,512]{3,2,1,0:T(8,128)(2,1)S(1)}, u32[]{:S(2)}, u32[]{:S(2)}) collective-permute-start(bf16[2,1,160,512]{3,2,1,0:T(8,128)(2,1)S(1)} %get-tuple-element.14), channel_id=1, source_target_pairs={{0,1},{1,2},{2,3},{3,4},{4,5},{5,6},{6,7},{7,8},{8,9},{9,10},{10,1... | collective-permute-start | bytes 983048 | tf_op jit(solution)/shard_map/ppermute | solution.py:20
  156.2 2.1 %collective-permute-start.2 = (bf16[2,1,160,512]{3,2,1,0:T(8,128)(2,1)S(1)}, bf16[2,1,160,512]{3,2,1,0:T(8,128)(2,1)S(1)}, u32[]{:S(2)}, u32[]{:S(2)}) collective-permute-start(bf16[2,1,160,512]{3,2,1,0:T(8,128)(2,1)S(1)} %get-tuple-element.15), channel_id=1, source_target_pairs={{1,0},{2,1},{3,2},{4,3},{5,4},{6,5},{7,6},{8,7},{9,8},{10,9},{11,1... | collective-permute-start | bytes 983048 | tf_op jit(solution)/shard_map/ppermute | solution.py:23
  158.3 3.8 %fusion.39 = (bf16[1,3,3,512,256]{4,3,2,1,0:T(8,128)(2,1)S(1)}, bf16[1,3,3,512,256]{4,3,2,1,0:T(8,128)(2,1)S(1)}, bf16[1,3,3,512,256]{4,3,2,1,0:T(8,128)(2,1)S(1)}) fusion(bf16[3,3,3,512,256]{4,3,2,1,0:T(8,128)(2,1)} %param.14), kind=kLoop, calls=%fused_computation.68 | loop fusion | bytes 14155776 | tf_op jit(solution)/shard_map/slice | solution.py:104
  162.1 0.2 fusion.46
  162.4 2.3 %collective-permute-done.2 = bf16[2,1,160,512]{3,2,1,0:T(8,128)(2,1)S(1)} collective-permute-done((bf16[2,1,160,512]{3,2,1,0:T(8,128)(2,1)S(1)}, bf16[2,1,160,512]{3,2,1,0:T(8,128)(2,1)S(1)}, u32[]{:S(2)}, u32[]{:S(2)}) %collective-permute-start.2) | collective-permute-done | bytes 327712 | tf_op jit(solution)/shard_map/ppermute | solution.py:23
  164.8 0.4 select_maximum_fusion
  165.9 0.4 fusion.40
  166.3 0.9 fusion.44
  167.3 0.9 fusion.45
  168.2 0.9 fusion.20
  169.1 0.9 fusion.21
  170.1 0.8 pad_maximum_fusion.5
  (34 shorter events, 1.7 us)
Async XLA Ops:
  6.5 78.9 %copy-start = (bf16[512,512]{1,0:T(8,128)(2,1)S(1)}, bf16[512,512]{1,0:T(8,128)(2,1)}, u32[]{:S(2)}) copy-start(bf16[512,512]{1,0:T(8,128)(2,1)} %param.10) | copy-start | bytes 1572868
  6.5 78.9 %all-gather.5.cloned.1.call-start = ((), (), s32[]{:S(2)}) async-start(), calls=%async_computation | async-start | bytes 5570560 | tf_op jit(solution)/shard_map/all_gather | solution.py:62
  35.8 96.6 %all-gather.7.cloned.1.call-start = ((), (), s32[]{:S(2)}) async-start(), calls=%async_computation.1 | async-start | bytes 5570560 | tf_op jit(solution)/shard_map/all_gather | solution.py:63
  92.8 39.6 %copy-start.1 = (bf16[1,2,160,512]{3,2,1,0:T(8,128)(2,1)S(1)}, bf16[1,2,160,512]{3,2,1,0:T(8,128)(2,1)}, u32[]{:S(2)}) copy-start(bf16[1,2,160,512]{3,2,1,0:T(8,128)(2,1)} %param.8) | copy-start | bytes 983044
  92.8 39.6 %copy-start.3 = (bf16[512,512]{1,0:T(8,128)(2,1)S(1)}, bf16[512,512]{1,0:T(8,128)(2,1)}, u32[]{:S(2)}) copy-start(bf16[512,512]{1,0:T(8,128)(2,1)} %param.13) | copy-start | bytes 1572868
  139.0 13.1 %collective-permute-start = (bf16[1,2,160,512]{3,2,1,0:T(8,128)(2,1)S(1)}, bf16[1,2,160,512]{3,2,1,0:T(8,128)(2,1)S(1)}, u32[]{:S(2)}, u32[]{:S(2)}) collective-permute-start(bf16[1,2,160,512]{3,2,1,0:T(8,128)(2,1)S(1)} %bitcast.54), channel_id=1, source_target_pairs={{0,16},{16,32},{32,48},{48,64},{64,80},{80,96},{96,112},{112,128},... | collective-permute-start | bytes 983048 | tf_op jit(solution)/shard_map/ppermute | solution.py:12
  152.2 10.2 %collective-permute-start.1 = (bf16[2,1,160,512]{3,2,1,0:T(8,128)(2,1)S(1)}, bf16[2,1,160,512]{3,2,1,0:T(8,128)(2,1)S(1)}, u32[]{:S(2)}, u32[]{:S(2)}) collective-permute-start(bf16[2,1,160,512]{3,2,1,0:T(8,128)(2,1)S(1)} %get-tuple-element.14), channel_id=1, source_target_pairs={{0,1},{1,2},{2,3},{3,4},{4,5},{5,6},{6,7},{7,8},{8,9},{9,10},{10,1... | collective-permute-start | bytes 983048 | tf_op jit(solution)/shard_map/ppermute | solution.py:20
  156.2 5.9 %copy-start.2 = (bf16[512,256]{1,0:T(8,128)(2,1)S(1)}, bf16[512,256]{1,0:T(8,128)(2,1)}, u32[]{:S(2)}) copy-start(bf16[512,256]{1,0:T(8,128)(2,1)} %param.15) | copy-start | bytes 786436
  156.2 8.5 %collective-permute-start.2 = (bf16[2,1,160,512]{3,2,1,0:T(8,128)(2,1)S(1)}, bf16[2,1,160,512]{3,2,1,0:T(8,128)(2,1)S(1)}, u32[]{:S(2)}, u32[]{:S(2)}) collective-permute-start(bf16[2,1,160,512]{3,2,1,0:T(8,128)(2,1)S(1)} %get-tuple-element.15), channel_id=1, source_target_pairs={{1,0},{2,1},{3,2},{4,3},{5,4},{6,5},{7,6},{8,7},{9,8},{10,9},{11,1... | collective-permute-start | bytes 983048 | tf_op jit(solution)/shard_map/ppermute | solution.py:23
Sparse Core Ops, SparseCore 0:
  35.9 49.4 all-gather.4
  87.6 44.7 all-gather.6
where the time goes:
time: 178 us
  waiting for transfers between devices  95.4 us (54%)
  blocking collectives  24.2 us (14%)
  matrix products  22.1 us (12%)
  between operations  13.6 us (8%)
  starting transfers between devices  9.19 us (5%)
  other arithmetic  7.78 us (4%)
  local copies, waits for them, and re-layouts  5.34 us (3%)
    all_gather x1, waiting for transfers between devices, per_device(): lax.all_gather(key_local, 'tile', axis=1, tiled=True)  47.5 us
    all_gather x1, waiting for transfers between devices, per_device(): lax.all_gather(value_local, 'tile', axis=1, tiled=True)  35.6 us
    psum x1, blocking collectives, per_device(): lax.psum((jnp.sum(grouped, axis=(1, 3)), jnp.sum(grouped * grouped, axis=...  24.2 us
    ppermute x1, waiting for transfers between devices, shifted(): return lax.ppermute(array, axis, pairs)  9.96 us
    dot_general x1, matrix products, per_device(): jnp.einsum('fqc,fkc->fqk', queries, key_rows, preferred_element_type=jnp....  7.33 us
    dot_general x1, matrix products, per_device(): jnp.einsum('fqc,cd->fqd', attended, out_weight, preferred_element_type=jn...  6.62 us
    ppermute x1, starting transfers between devices, padded_2(): lax.ppermute(lax.slice_in_dim(block, block.shape[dim] - width, None, axis...  4 us
    reduce_sum x1, other arithmetic, per_device(): denominator = jnp.sum(unnormed, axis=2, keepdims=True)  3.96 us
  transfers between devices with their start and end apart: 5, of which 4 were waited for; matrix products, arithmetic and copies ran while one was open for 10% of the time, Pallas kernels for 0%

commit v1 on v0

--- a/solution.py
+++ b/solution.py
@@ -4,6 +4,11 @@
 from jax.sharding import PartitionSpec as P
 
 GROUPS = 32
+
+
+def swapped_in(shard, mesh_axis, dim):
+    sent = jnp.stack([shard] * lax.axis_size(mesh_axis))
+    return jnp.concatenate(lax.all_to_all(sent, mesh_axis, 0, 0), axis=dim)
 
 
 def shifted(array, axis, by):
@@ -59,7 +64,7 @@
         "fnc,cd->fnd", normed, value_weight, preferred_element_type=jnp.float32
     ).astype(jnp.bfloat16)
     key_rows, value_rows = (
-        lax.all_gather(key_local, "tile", axis=1, tiled=True),
+        swapped_in(key_local, "tile", 1),
         lax.all_gather(value_local, "tile", axis=1, tiled=True),
     )
     scores = jnp.einsum(

time: 178 us -> 245 us (1.38)
  the two profiles are of different devices: /device:TPU:65 before, /device:TPU:281 now
where the time goes in v1:
time: 245 us; the launch traced here: 244 us
  waiting for transfers between devices  154 us (63%)
  blocking collectives  23.1 us (9%)
  matrix products  20.3 us (8%)
  starting transfers between devices  17 us (7%)
  between operations  13.7 us (6%)
  local copies, waits for them, and re-layouts  8.17 us (3%)
  other arithmetic  7.78 us (3%)
    all_to_all x1, waiting for transfers between devices, swapped_in(): return jnp.concatenate(lax.all_to_all(sent, mesh_axis, 0, 0), axis=dim)  140 us
    psum x1, blocking collectives, per_device(): lax.psum((jnp.sum(grouped, axis=(1, 3)), jnp.sum(grouped * grouped, axis=...  23.1 us
    ppermute x1, waiting for transfers between devices, shifted(): return lax.ppermute(array, axis, pairs)  11 us
    all_to_all x1, starting transfers between devices, swapped_in(): return jnp.concatenate(lax.all_to_all(sent, mesh_axis, 0, 0), axis=dim)  8.34 us
    dot_general x1, matrix products, per_device(): jnp.einsum('fqc,fkc->fqk', queries, key_rows, preferred_element_type=jnp....  7.33 us
    dot_general x1, matrix products, per_device(): jnp.einsum('fqc,cd->fqd', attended, out_weight, preferred_element_type=jn...  6.62 us
  transfers between devices with their start and end apart: 5, of which 3 were waited for; matrix products, arithmetic and copies ran while one was open for 7% of the time, Pallas kernels for 0%

profile of v1, /device:TPU:281, one launch (start us, length us, event | category | flops | bytes accessed | tf_op | source)
XLA Modules:
  0.0 244.2 jit_solution(15206562786482067654)
XLA Ops:
  6.5 1.1 convert_reduce_fusion
  8.1 23.1 %all-reduce.1 = (f32[1,32]{1,0:T(1,128)S(1)}, f32[1,32]{1,0:T(1,128)S(1)}) all-reduce(f32[1,32]{1,0:T(1,128)S(1)} %bitcast.68, f32[1,32]{1,0:T(1,128)S(1)} %bitcast.67), channel_id=1, replica_groups=mesh['tm'=32,'tile'=16] {'tile'}, use_global_device_ids=true, to_apply=%region_5.0 | all-reduce | flops 64 | bytes 512 | tf_op jit(solution)/shard_map/psum | solution.py:47
  31.5 1.1 fusion.33
  32.6 1.4 convolution_convert_fusion.1
  34.0 2.8 %stack.8 = bf16[16,1,320,512]{3,2,1,0:T(8,128)(2,1)} broadcast(bf16[320,512]{1,0:T(8,128)(2,1)S(1)} %convolution_convert_fusion.1), dimensions={2,3} | broadcast | bytes 5570560 | tf_op jit(solution)/shard_map/stack | solution.py:10
  36.8 8.3 %all-to-all-start = ((bf16[16,1,320,512]{3,2,1,0:T(8,128)(2,1)}), bf16[16,1,320,512]{3,2,1,0:T(8,128)(2,1)}, u32[]{:S(2)}, u32[]{:S(2)}) async-start(bf16[16,1,320,512]{3,2,1,0:T(8,128)(2,1)} %stack.8), calls=%async_computation | async-start | bytes 10485760 | tf_op jit(solution)/shard_map/all_to_all | solution.py:11
  45.2 1.1 convolution_convert_fusion
  46.3 139.6 %all-to-all-done = bf16[16,1,320,512]{3,2,1,0:T(8,128)(2,1)} async-done(((bf16[16,1,320,512]{3,2,1,0:T(8,128)(2,1)}), bf16[16,1,320,512]{3,2,1,0:T(8,128)(2,1)}, u32[]{:S(2)}, u32[]{:S(2)}) %all-to-all-start) | async-done | bytes 5242912 | tf_op jit(solution)/shard_map/all_to_all | solution.py:11
  185.9 7.3 %fusion.41 = (f32[320]{0:T(512)S(1)}, f32[320,5120]{1,0:T(8,128)}) fusion(bf16[5120,512]{1,0:T(8,128)(2,1)} %bitcast.5, bf16[320,512]{1,0:T(8,128)(2,1)S(1)} %fusion.33, bf16[512,512]{1,0:T(8,128)(2,1)S(1)} %copy-done), kind=kOutput, calls=%fused_computation.70 | convolution fusion | flops 1848934144 | bytes 12649728 | tf_op jit(solution)/shard_map/fqc,fkc->fqk/dot_general | solution.py:70
  193.3 4.0 %fusion = f32[320]{0:T(512)S(1)} fusion(f32[320,5120]{1,0:T(8,128)} %get-tuple-element.17, f32[320]{0:T(512)S(1)} %get-tuple-element.16), kind=kLoop, calls=%fused_computation.2 | loop fusion | flops 3276480 | bytes 6556160 | tf_op jit(solution)/shard_map/reduce_sum | solution.py:75
  197.3 6.6 %fusion.27 = (bf16[320,512]{1,0:T(8,128)(2,1)S(1)}, bf16[320,512]{1,0:T(8,128)(2,1)S(1)}) fusion(bf16[512,512]{1,0:T(8,128)(2,1)S(1)} %copy-done.4, bf16[5120,512]{1,0:T(8,128)(2,1)} %all-gather.3.cloned.1.call-done, f32[320,5120]{1,0:T(8,128)} %get-tuple-element.17, f32[320]{0:T(512)S(1)} %get-tuple-element.16, f32[320]{0:T(512)S(1)} %fusion, ...), kind=kOutput, calls=%fused_computation.39 | convolution fusion | flops 1850572800 | bytes 13306368 | tf_op jit(solution)/shard_map/fqc,cd->fqd/dot_general | solution.py:81
  203.9 3.1 %collective-permute-start = (bf16[1,2,160,512]{3,2,1,0:T(8,128)(2,1)S(1)}, bf16[1,2,160,512]{3,2,1,0:T(8,128)(2,1)S(1)}, u32[]{:S(2)}, u32[]{:S(2)}) collective-permute-start(bf16[1,2,160,512]{3,2,1,0:T(8,128)(2,1)S(1)} %bitcast.55), channel_id=1, source_target_pairs={{0,16},{16,32},{32,48},{48,64},{64,80},{80,96},{96,112},{112,128},... | collective-permute-start | bytes 983048 | tf_op jit(solution)/shard_map/ppermute | solution.py:17
  207.1 11.0 %collective-permute-done = bf16[1,2,160,512]{3,2,1,0:T(8,128)(2,1)S(1)} collective-permute-done((bf16[1,2,160,512]{3,2,1,0:T(8,128)(2,1)S(1)}, bf16[1,2,160,512]{3,2,1,0:T(8,128)(2,1)S(1)}, u32[]{:S(2)}, u32[]{:S(2)}) %collective-permute-start) | collective-permute-done | bytes 327712 | tf_op jit(solution)/shard_map/ppermute | solution.py:17
  218.1 3.4 %collective-permute-start.1 = (bf16[2,1,160,512]{3,2,1,0:T(8,128)(2,1)S(1)}, bf16[2,1,160,512]{3,2,1,0:T(8,128)(2,1)S(1)}, u32[]{:S(2)}, u32[]{:S(2)}) collective-permute-start(bf16[2,1,160,512]{3,2,1,0:T(8,128)(2,1)S(1)} %get-tuple-element.14), channel_id=1, source_target_pairs={{0,1},{1,2},{2,3},{3,4},{4,5},{5,6},{6,7},{7,8},{8,9},{9,10},{10,1... | collective-permute-start | bytes 983048 | tf_op jit(solution)/shard_map/ppermute | solution.py:25
  221.5 2.1 collective-permute-start.2
  223.6 3.8 %fusion.39 = (bf16[1,3,3,512,256]{4,3,2,1,0:T(8,128)(2,1)S(1)}, bf16[1,3,3,512,256]{4,3,2,1,0:T(8,128)(2,1)S(1)}, bf16[1,3,3,512,256]{4,3,2,1,0:T(8,128)(2,1)S(1)}) fusion(bf16[3,3,3,512,256]{4,3,2,1,0:T(8,128)(2,1)} %param.14), kind=kLoop, calls=%fused_computation.68 | loop fusion | bytes 14155776 | tf_op jit(solution)/shard_map/slice | solution.py:109
  227.7 3.5 %collective-permute-done.2 = bf16[2,1,160,512]{3,2,1,0:T(8,128)(2,1)S(1)} collective-permute-done((bf16[2,1,160,512]{3,2,1,0:T(8,128)(2,1)S(1)}, bf16[2,1,160,512]{3,2,1,0:T(8,128)(2,1)S(1)}, u32[]{:S(2)}, u32[]{:S(2)}) %collective-permute-start.2) | collective-permute-done | bytes 327712 | tf_op jit(solution)/shard_map/ppermute | solution.py:28
  231.3 0.4 select_maximum_fusion
  232.5 0.4 fusion.40
  232.9 0.9 fusion.44
  233.8 0.9 fusion.45
  234.7 0.9 fusion.20
  235.7 0.9 fusion.21
  236.6 0.8 pad_maximum_fusion.5
  (36 shorter events, 1.9 us)
Async XLA Ops:
  6.5 179.4 %copy-start = (bf16[512,512]{1,0:T(8,128)(2,1)S(1)}, bf16[512,512]{1,0:T(8,128)(2,1)}, u32[]{:S(2)}) copy-start(bf16[512,512]{1,0:T(8,128)(2,1)} %param.10) | copy-start | bytes 1572868
  36.8 8.4 %copy-start.2 = (bf16[512,512]{1,0:T(8,128)(2,1)S(1)}, bf16[512,512]{1,0:T(8,128)(2,1)}, u32[]{:S(2)}) copy-start(bf16[512,512]{1,0:T(8,128)(2,1)} %param.12) | copy-start | bytes 1572868
  36.8 149.1 %all-to-all-start = ((bf16[16,1,320,512]{3,2,1,0:T(8,128)(2,1)}), bf16[16,1,320,512]{3,2,1,0:T(8,128)(2,1)}, u32[]{:S(2)}, u32[]{:S(2)}) async-start(bf16[16,1,320,512]{3,2,1,0:T(8,128)(2,1)} %stack.8), calls=%async_computation | async-start | bytes 10485760 | tf_op jit(solution)/shard_map/all_to_all | solution.py:11
  45.2 152.1 %all-gather.3.cloned.1.call-start = ((), (), s32[]{:S(2)}) async-start(), calls=%async_computation.1 | async-start | bytes 5570560 | tf_op jit(solution)/shard_map/all_gather | solution.py:68
  193.3 4.0 %copy-start.1 = (bf16[1,2,160,512]{3,2,1,0:T(8,128)(2,1)S(1)}, bf16[1,2,160,512]{3,2,1,0:T(8,128)(2,1)}, u32[]{:S(2)}) copy-start(bf16[1,2,160,512]{3,2,1,0:T(8,128)(2,1)} %param.8) | copy-start | bytes 983044
  193.3 4.0 %copy-start.4 = (bf16[512,512]{1,0:T(8,128)(2,1)S(1)}, bf16[512,512]{1,0:T(8,128)(2,1)}, u32[]{:S(2)}) copy-start(bf16[512,512]{1,0:T(8,128)(2,1)} %param.13) | copy-start | bytes 1572868
  203.9 14.1 %collective-permute-start = (bf16[1,2,160,512]{3,2,1,0:T(8,128)(2,1)S(1)}, bf16[1,2,160,512]{3,2,1,0:T(8,128)(2,1)S(1)}, u32[]{:S(2)}, u32[]{:S(2)}) collective-permute-start(bf16[1,2,160,512]{3,2,1,0:T(8,128)(2,1)S(1)} %bitcast.55), channel_id=1, source_target_pairs={{0,16},{16,32},{32,48},{48,64},{64,80},{80,96},{96,112},{112,128},... | collective-permute-start | bytes 983048 | tf_op jit(solution)/shard_map/ppermute | solution.py:17
  218.1 9.6 %collective-permute-start.1 = (bf16[2,1,160,512]{3,2,1,0:T(8,128)(2,1)S(1)}, bf16[2,1,160,512]{3,2,1,0:T(8,128)(2,1)S(1)}, u32[]{:S(2)}, u32[]{:S(2)}) collective-permute-start(bf16[2,1,160,512]{3,2,1,0:T(8,128)(2,1)S(1)} %get-tuple-element.14), channel_id=1, source_target_pairs={{0,1},{1,2},{2,3},{3,4},{4,5},{5,6},{6,7},{7,8},{8,9},{9,10},{10,1... | collective-permute-start | bytes 983048 | tf_op jit(solution)/shard_map/ppermute | solution.py:25
  221.5 5.9 %copy-start.3 = (bf16[512,256]{1,0:T(8,128)(2,1)S(1)}, bf16[512,256]{1,0:T(8,128)(2,1)}, u32[]{:S(2)}) copy-start(bf16[512,256]{1,0:T(8,128)(2,1)} %param.15) | copy-start | bytes 786436
  221.5 9.7 %collective-permute-start.2 = (bf16[2,1,160,512]{3,2,1,0:T(8,128)(2,1)S(1)}, bf16[2,1,160,512]{3,2,1,0:T(8,128)(2,1)S(1)}, u32[]{:S(2)}, u32[]{:S(2)}) collective-permute-start(bf16[2,1,160,512]{3,2,1,0:T(8,128)(2,1)S(1)} %get-tuple-element.15), channel_id=1, source_target_pairs={{1,0},{2,1},{3,2},{4,3},{5,4},{6,5},{7,6},{8,7},{9,8},{10,9},{11,1... | collective-permute-start | bytes 983048 | tf_op jit(solution)/shard_map/ppermute | solution.py:28
Sparse Core Ops, SparseCore 0:
  48.1 128.3 all-gather.2
